TPU v7x, 256 devices: a whole 4x4x8 slice. The times are simulated.
256 devices in a mesh: rows: 64 (over y, z, core), cols: 4 (over x).
Axes of the slice: x: 4, y: 4, z: 8, core: 2. Of those that a mesh axis runs over, the one named last changes fastest.
Arguments:
- inner_pivots: float32 [3072, 128, 128], P(('rows', 'cols')), may hold values from 0 to 4, as said below
- lower_blocks: float32 [3072, 4, 128, 128], P('rows', 'cols'), may hold values from -0.13 to 0.13
- upper_blocks: float32 [3072, 4, 128, 128], P('rows', 'cols'), may hold values from -0.13 to 0.13
- separator_pivots: float32 [64, 128, 128], P('rows', 'cols'), may hold values from 0 to 16, as said below
- separator_ids: int32 [3072, 4], P('rows', 'cols'), may hold values from 0 to 63, all different within a row
- coupling_count: int32 [3072], P('rows'), may hold values from 1 to 4
Outputs:
- inner_inverse: float32 [3072, 128, 128], P(('rows', 'cols'))
- lower_factor: float32 [3072, 4, 128, 128], P('rows', 'cols')
- separator_inverse: float32 [64, 128, 128], P('rows', 'cols')
Inputs may be any that keep to these rules, and one draw needn't show every extreme that they name: `inner_pivots`: each row's diagonal entry is positive and larger than the sum of the magnitudes of the row's other entries. `separator_pivots`: each row's diagonal entry is positive and larger than the sum of the magnitudes of the row's other entries. `separator_ids`: the 4 slots of an interior name different separators; every separator is named by some slot. Interior i couples through its first coupling_count[i] slots only.
All inputs are finite; a program needn't handle non-finite values.
Results may differ from a plain program's by a relative error of at most 0.0001.
Values sent between devices are 32-bit elements; how exact they have to be, the bound alone decides.
A program may use at most 64 MiB of HBM per device.

v0:
```python
import functools

import jax
import jax.numpy as jnp
from jax import lax
from jax.experimental import pallas as pl
from jax.experimental.pallas import tpu as pltpu
from jax.sharding import PartitionSpec as P

HIGH = lax.Precision.HIGH
VMEM = pl.BlockSpec(memory_space=pltpu.VMEM)
SMEM = pl.BlockSpec(memory_space=pltpu.SMEM)
GRANT = 48 << 20


def dot(a, b):
    return lax.dot_general(a, b, (((1,), (0,)), ((), ())), precision=HIGH, preferred_element_type=jnp.float32)


def eliminate(slabs, first, ahead):
    depth, width = slabs[0].shape
    lanes = lax.broadcasted_iota(jnp.int32, (1, width), 1)
    rows = lax.broadcasted_iota(jnp.int32, (depth, width), 0)
    for start in range(0, depth, ahead):
        base = first + start
        spread = [
            [jnp.broadcast_to(slab[:, base + t : base + t + 1], (depth, width)) for t in range(ahead)]
            for slab in slabs
        ]
        for t in range(ahead):
            k = start + t
            at_lane = (lanes == base + t).astype(jnp.float32)
            at_row = (rows == k).astype(jnp.float32)
            for index, slab in enumerate(slabs):
                columns = spread[index]
                inverse = 1.0 / columns[t][k : k + 1, :]
                pivot_row = (slab[k : k + 1, :] + at_lane) * inverse
                column = columns[t] - at_row
                for u in range(t + 1, ahead):
                    columns[u] = columns[u] - column * (columns[u][k : k + 1, :] * inverse)
                slabs[index] = slab - column * pivot_row
    return slabs


def invert(ref, members, panel, ahead):
    size = ref.shape[-1]
    lanes = lax.broadcasted_iota(jnp.int32, (1, size), 1)
    for first in range(0, size, panel):
        slabs = eliminate([ref[b, first : first + panel, :] for b in members], first, ahead)
        inside = (lanes >= first) & (lanes < first + panel)
        for b, slab in zip(members, slabs):
            whole = ref[b]
            update = dot(whole[:, first : first + panel], slab)
            ref[b] = jnp.where(inside, 0.0, whole) - update
            ref[b, first : first + panel, :] = slab


def interiors_kernel(pivots, out):
    out[...] = pivots[...]
    invert(out, range(pivots.shape[0]), 8, 8)


def couplings_kernel(group, first_slot, ids, counts, inverses, lower, upper, factor, schur):
    step = pl.program_id(0)

    @pl.when(step == 0)
    def _():
        schur[...] = jnp.zeros_like(schur)

    products = []
    for g in range(group):
        live = first_slot[0] < counts[step * group + g]
        value = jnp.where(live, dot(lower[g, 0], inverses[g]), 0.0)
        factor[g, 0] = value
        products.append(dot(value, upper[g, 0]))
    for g in range(group):
        j = ids[step * group + g]
        schur[j] = schur[j] + products[g]


def separator_kernel(pivots, total, own, out, work):
    work[0] = pivots[...] - total[...]
    invert(work, range(1), 32, 16)
    rows = out.shape[0]
    out[...] = work[0, pl.ds(pl.multiple_of(own[0] * rows, rows), rows), :]


def shards(inner_pivots, lower_blocks, upper_blocks, separator_pivots, separator_ids, coupling_count):
    f32 = jnp.float32
    count, size = inner_pivots.shape[0], inner_pivots.shape[1]
    couplings = lower_blocks.shape[0]
    col = lax.axis_index("cols").astype(jnp.int32)
    separators = separator_pivots.shape[0] * lax.axis_size("rows")
    params = pltpu.CompilerParams(vmem_limit_bytes=GRANT)

    inner_inverse = pl.pallas_call(
        interiors_kernel,
        out_shape=jax.ShapeDtypeStruct((count, size, size), f32),
        in_specs=[VMEM],
        out_specs=VMEM,
        compiler_params=params,
    )(inner_pivots)
    inverses = lax.all_gather(inner_inverse, "cols", axis=0, tiled=True)

    group = 6
    block = pl.BlockSpec((group, 1, size, size), lambda s, *_: (s, 0, 0, 0))
    lower_factor, schur = pl.pallas_call(
        functools.partial(couplings_kernel, group),
        grid_spec=pltpu.PrefetchScalarGridSpec(
            num_scalar_prefetch=3,
            grid=(couplings // group,),
            in_specs=[pl.BlockSpec((group, size, size), lambda s, *_: (s, 0, 0)), block, block],
            out_specs=[block, pl.BlockSpec((separators, size, size), lambda s, *_: (0, 0, 0))],
        ),
        out_shape=[
            jax.ShapeDtypeStruct(lower_blocks.shape, f32),
            jax.ShapeDtypeStruct((separators, size, size), f32),
        ],
        compiler_params=params,
    )(col[None], separator_ids.reshape(-1), coupling_count, inverses, lower_blocks, upper_blocks)

    summed = lax.psum_scatter(schur, "rows", scatter_dimension=0, tiled=True)
    summed = lax.psum(summed, "cols")
    pivots = lax.all_gather(separator_pivots, "cols", axis=1, tiled=True)
    own = pl.pallas_call(
        separator_kernel,
        out_shape=jax.ShapeDtypeStruct(separator_pivots.shape[1:], f32),
        in_specs=[VMEM, VMEM, SMEM],
        out_specs=VMEM,
        scratch_shapes=[pltpu.VMEM((1, size, size), f32)],
        compiler_params=params,
    )(pivots[0], summed[0], col[None])
    return inner_inverse, lower_factor, own[None]


def solution(mesh):
    placed = (
        P(("rows", "cols"), None, None),
        P("rows", "cols", None, None),
        P("rows", "cols", None, None),
        P("rows", "cols", None),
        P("rows", "cols"),
        P("rows"),
    )
    return jax.shard_map(
        shards,
        mesh=mesh,
        in_specs=placed,
        out_specs=(
            P(("rows", "cols"), None, None),
            P("rows", "cols", None, None),
            P("rows", "cols", None),
        ),
        check_vma=False,
    )
```

profile of v0, /device:TPU:2, one launch (start us, length us, event | category | flops | bytes accessed | tf_op | source)
XLA Modules:
  0.0 277.3 jit_solution(3833076567897802132)
XLA Ops:
  7.2 0.0 all-gather.2.cloned.1.call-start
  7.2 0.0 copy-start.1
  7.2 1.1 copy-done.1
  8.3 9.3 %shard_map.85 = f32[12,128,128]{2,1,0:T(8,128)} custom-call(f32[12,128,128]{2,1,0:T(8,128)S(1)} %copy-done.1), custom_call_target="tpu_custom_call" | custom-call | tf_op jit(solution)/shard_map/pallas_call | solution.py:96
  17.6 0.0 all-gather.2.cloned.1.call-update
  17.6 0.0 reduce-scatter.2.cloned.1.call-start
  17.7 44.4 %all-gather.2.cloned.1.call-done.inverses = f32[48,128,128]{2,1,0:T(8,128)} async-done(((f32[12,128,128]{2,1,0:T(8,128)}), f32[48,128,128]{2,1,0:T(8,128)}) %all-gather.2.cloned.1.call-update) | async-done | bytes 3145744 | tf_op jit(solution)/shard_map/all_gather | solution.py:103
  62.0 0.0 copy-start
  62.0 1.9 copy-done
  63.9 0.0 copy-start.3
  63.9 0.7 copy-done.3
  64.6 0.0 copy-start.4
  64.6 0.7 copy-done.4
  65.2 10.5 %shard_map.86 = (f32[48,1,128,128]{3,2,1,0:T(8,128)}, f32[64,128,128]{2,1,0:T(8,128)}) custom-call(s32[1]{0:T(128)} %bitcast.first_slot.own, s32[48]{0:T(128)S(1)} %bitcast.6, s32[48]{0:T(128)S(1)} %copy-done.4, f32[48,128,128]{2,1,0:T(8,128)S(1)} %copy-done, f32[48,1,128,128]{3,2,1,0:T(8,128)} %lower.1, f32[48,1,128,128]{3,2,1,0:T(8,128)} %upper.1), custom_call_target="tpu_custom_call" | custom-call | tf_op jit(solution)/shard_map/pallas_call | solution.py:107
  75.7 0.0 copy-start.5
  75.7 0.0 reduce-scatter.2.cloned.1.call-update
  75.7 0.0 all-reduce.2.cloned.1.call-start
  75.8 145.0 %reduce-scatter.2.cloned.1.call-done = f32[1,128,128]{2,1,0:T(8,128)} async-done(((f32[64,128,128]{2,1,0:T(8,128)}), f32[1,128,128]{2,1,0:T(8,128)}) %reduce-scatter.2.cloned.1.call-update) | async-done | bytes 65552 | tf_op jit(solution)/shard_map/reduce_scatter | solution.py:122
  220.8 0.0 all-reduce.2.cloned.1.call-update
  220.8 0.0 copy-done.5
  220.8 12.1 %all_gather.7 = f32[1,128,128]{2,1,0:T(8,128)S(1)} all-gather(f32[1,32,128]{2,1,0:T(8,128)S(1)} %copy-done.5), channel_id=1, replica_groups=mesh['rows'=64,'cols'=4] {'cols'}, dimensions={1}, use_global_device_ids=true | all-gather | bytes 81920 | tf_op jit(solution)/shard_map/all_gather | solution.py:124
  232.9 33.3 %all-reduce.2.cloned.1.call-done.total = f32[128,128]{1,0:T(8,128)} async-done(((f32[128,128]{1,0:T(8,128)}), f32[128,128]{1,0:T(8,128)}) %all-reduce.2.cloned.1.call-update) | async-done | bytes 65552 | tf_op jit(solution)/shard_map/psum | solution.py:123
  266.2 0.0 copy-start.2
  266.3 0.8 copy-done.2
  267.1 3.7 %shard_map.87 = f32[32,128]{1,0:T(8,128)} custom-call(f32[128,128]{1,0:T(8,128)S(1)} %bitcast.5, f32[128,128]{1,0:T(8,128)S(1)} %copy-done.2, s32[1]{0:T(128)} %bitcast.first_slot.own), custom_call_target="tpu_custom_call" | custom-call | tf_op jit(solution)/shard_map/pallas_call | solution.py:125
Async XLA Ops:
  7.2 54.9 %all-gather.2.cloned.1.call-start = ((), (), s32[]{:S(2)}) async-start(), calls=%async_computation.1 | async-start | bytes 3932160 | tf_op jit(solution)/shard_map/all_gather | solution.py:103
  7.2 1.1 copy-start.1
  17.6 203.2 %reduce-scatter.2.cloned.1.call-start = ((), (), s32[]{:S(2)}) async-start(), calls=%async_computation.2 | async-start | bytes 4259840 | tf_op jit(solution)/shard_map/reduce_scatter | solution.py:122
  62.0 1.9 copy-start
  63.9 0.7 copy-start.3
  64.6 0.7 copy-start.4
  75.7 145.1 %copy-start.5 = (f32[1,32,128]{2,1,0:T(8,128)S(1)}, f32[1,32,128]{2,1,0:T(8,128)}, u32[]{:S(2)}) copy-start(f32[1,32,128]{2,1,0:T(8,128)} %param.9) | copy-start | bytes 49156
  75.7 190.5 %all-reduce.2.cloned.1.call-start = ((), (), s32[]{:S(2)}) async-start(), calls=%async_computation.3 | async-start | bytes 131072 | tf_op jit(solution)/shard_map/psum | solution.py:123
  266.2 0.8 copy-start.2
Sparse Core Ops, SparseCore 0:
  17.8 44.2 all-gather.1
  75.8 144.8 reduce-scatter.1
  223.2 43.0 all-reduce.1
where the time goes:
time: 279 us; the launch traced here: 277 us
  waiting for transfers between devices  223 us (80%)
  Pallas kernels  23.4 us (8%)
  between operations  13.8 us (5%)
  blocking collectives  12.1 us (4%)
  local copies, waits for them, and re-layouts  5.17 us (2%)
    reduce_scatter x1, waiting for transfers between devices, shards(): summed = lax.psum_scatter(schur, 'rows', scatter_dimension=0, tiled=True)  145 us
    all_gather x1, waiting for transfers between devices, shards(): inverses = lax.all_gather(inner_inverse, 'cols', axis=0, tiled=True)  44.4 us
    psum x1, waiting for transfers between devices, shards(): summed = lax.psum(summed, 'cols')  33.3 us
    all_gather x1, blocking collectives, shards(): pivots = lax.all_gather(separator_pivots, 'cols', axis=1, tiled=True)  12.1 us
    pallas_call x1, Pallas kernels, shards(): pl.pallas_call(functools.partial(couplings_kernel, group), grid_spec=pltp...  10.5 us
    pallas_call x1, Pallas kernels, shards(): pl.pallas_call(interiors_kernel, out_shape=jax.ShapeDtypeStruct((count, s...  9.26 us
  transfers between devices with their start and end apart: 3, of which 3 were waited for; matrix products, arithmetic and copies ran while one was open for 0% of the time, Pallas kernels for 0%

commit v1 on v0

--- a/solution.py
+++ b/solution.py
@@ -11,6 +11,7 @@
 VMEM = pl.BlockSpec(memory_space=pltpu.VMEM)
 SMEM = pl.BlockSpec(memory_space=pltpu.SMEM)
 GRANT = 48 << 20
+CORES, RING, DEPTH, TILE = 2, 4, 8, 8
 
 
 def dot(a, b):
@@ -75,14 +76,192 @@
         products.append(dot(value, upper[g, 0]))
     for g in range(group):
         j = ids[step * group + g]
-        schur[j] = schur[j] + products[g]
-
-
-def separator_kernel(pivots, total, own, out, work):
-    work[0] = pivots[...] - total[...]
-    invert(work, range(1), 32, 16)
-    rows = out.shape[0]
-    out[...] = work[0, pl.ds(pl.multiple_of(own[0] * rows, rows), rows), :]
+        core, spot = lax.rem(j, CORES), lax.div(j, CORES)
+        for quarter in range(RING):
+            for half in range(2):
+                for way in range(2):
+                    row = quarter * 32 + half * 16 + way * TILE
+                    at = (core, half, way, quarter, spot)
+                    schur[at] = schur[at] + products[g][row : row + TILE, :]
+
+
+class Ring:
+    def __init__(self, axis, step, me, blocks, own, land, send, recv):
+        self.blocks, self.own, self.land, self.send, self.recv = blocks, own, land, send, recv
+        self.me, self.axis, self.step = me, axis, step
+        self.sent = []
+
+    def at(self, offset):
+        return lax.rem(self.me + offset, RING)
+
+    def copy(self, slot, source, offset):
+        copy = pltpu.make_async_remote_copy(
+            src_ref=source,
+            dst_ref=self.land.at[slot],
+            send_sem=self.send.at[slot],
+            recv_sem=self.recv.at[slot],
+            device_id=self.step(self.at(offset)),
+            device_id_type=pl.DeviceIdType.MESH,
+        )
+        copy.start()
+        self.sent.append(copy)
+        return copy
+
+    def first(self):
+        self.relay_up = self.copy(0, self.blocks(1, self.at(2)), 1)
+        self.relay_down = self.copy(1, self.blocks(0, self.at(2)), 3)
+        self.last_up = self.copy(2, self.blocks(0, self.at(1)), 1)
+        self.last_down = self.copy(3, self.blocks(1, self.at(3)), 3)
+
+    def second(self):
+        self.relay_up.wait_recv()
+        block = self.blocks(1, self.at(1))
+        block[...] = block[...] + self.land[0]
+        self.sum_up = self.copy(4, block, 1)
+        self.relay_down.wait_recv()
+        block = self.blocks(0, self.at(3))
+        block[...] = block[...] + self.land[1]
+        self.sum_down = self.copy(5, block, 3)
+
+    def third(self):
+        self.last_up.wait_recv()
+        self.sum_down.wait_recv()
+        self.own(0, self.blocks(0, self.me)[...] + (self.land[2] + self.land[5]))
+        self.last_down.wait_recv()
+        self.sum_up.wait_recv()
+        self.own(1, self.blocks(1, self.me)[...] + (self.land[3] + self.land[4]))
+
+    def drain(self):
+        for copy in self.sent:
+            copy.wait_send()
+
+
+def separators_kernel(
+    schur, pivots, out, mine, other, x_wide, y_wide, x_part, y_part, x_thin, y_thin, stack, column, work, whole,
+    send, recv, load, core_send, core_recv, z_send, z_recv, q_send, q_recv,
+):
+    row, x = lax.axis_index("rows"), lax.axis_index("cols")
+    core = lax.rem(row, CORES)
+    z = lax.rem(lax.div(row, CORES), DEPTH)
+    y = lax.div(row, CORES * DEPTH)
+
+    def device(x_at, y_at, z_at, core_at):
+        return {"rows": (y_at * DEPTH + z_at) * CORES + core_at, "cols": x_at}
+
+    sibling = device(x, y, z, 1 - core)
+    along_x = lambda at: device(at, y, z, core)
+    along_y = lambda at: device(x, at, z, core)
+    along_z = lambda at: device(x, y, at, core)
+
+    barrier = pltpu.get_barrier_semaphore()
+    greeted = [sibling]
+    greeted += [along_x(lax.rem(x + t, RING)) for t in (1, 2, 3)]
+    greeted += [along_y(lax.rem(y + t, RING)) for t in (1, 3)]
+    greeted += [along_z(lax.rem(z + t, DEPTH)) for t in range(1, DEPTH)]
+    for peer in greeted:
+        pl.semaphore_signal(barrier, inc=1, device_id=peer, device_id_type=pl.DeviceIdType.MESH)
+
+    loads = []
+    for part in range(4):
+        half, way = part // 2, part % 2
+        copy = pltpu.make_async_copy(schur.at[core, half, way], mine.at[half, way], load.at[part])
+        copy.start()
+        loads.append(copy)
+    pl.semaphore_wait(barrier, len(greeted))
+
+    crossed = []
+    for part in range(4):
+        half, way = part // 2, part % 2
+        copy = pltpu.make_async_remote_copy(
+            src_ref=schur.at[1 - core, half, way],
+            dst_ref=other.at[half, way],
+            send_sem=core_send.at[part],
+            recv_sem=core_recv.at[part],
+            device_id=sibling,
+            device_id_type=pl.DeviceIdType.MESH,
+        )
+        copy.start()
+        crossed.append(copy)
+    for part in range(4):
+        half, way = part // 2, part % 2
+        loads[part].wait()
+        crossed[part].wait_recv()
+        mine[half, way] = mine[half, way] + other[half, way]
+
+    def keep_x(way, value):
+        x_part[way] = value
+
+    def keep_y(way, value):
+        y_part[way] = value
+
+    wide_x = Ring("x", along_x, x, lambda way, d: mine.at[0, way, d], keep_x, x_wide, send.at[0], recv.at[0])
+    wide_y = Ring(
+        "y", along_y, y, lambda way, d: mine.at[1, way, :, pl.ds(d * DEPTH, DEPTH)], keep_y, y_wide,
+        send.at[1], recv.at[1],
+    )
+    for stage in ("first", "second", "third"):
+        getattr(wide_x, stage)()
+        getattr(wide_y, stage)()
+
+    def stack_x(way, value):
+        for t in range(DEPTH):
+            stack[t, way] = value[t]
+
+    def stack_y(way, value):
+        for t in range(DEPTH):
+            stack[t, 2 + way] = value[t]
+
+    thin_y = Ring(
+        "y", along_y, y, lambda way, d: x_part.at[way, pl.ds(d * DEPTH, DEPTH)], stack_x, y_thin,
+        send.at[2], recv.at[2],
+    )
+    thin_x = Ring("x", along_x, x, lambda way, d: y_part.at[way, d], stack_y, x_thin, send.at[3], recv.at[3])
+    for stage in ("first", "second", "third"):
+        getattr(thin_y, stage)()
+        getattr(thin_x, stage)()
+
+    spread = []
+    for t in range(1, DEPTH):
+        to = lax.rem(z + t, DEPTH)
+        copy = pltpu.make_async_remote_copy(
+            src_ref=stack.at[to],
+            dst_ref=column.at[t - 1],
+            send_sem=z_send.at[t - 1],
+            recv_sem=z_recv.at[t - 1],
+            device_id=along_z(to),
+            device_id_type=pl.DeviceIdType.MESH,
+        )
+        copy.start()
+        spread.append(copy)
+    total = stack[z]
+    for t in range(1, DEPTH):
+        spread[t - 1].wait_recv()
+        total = total + column[t - 1]
+
+    rows = pivots.shape[0]
+    work[x] = pivots[...] - total.reshape(rows, total.shape[-1])
+    quarters = []
+    for t in range(1, RING):
+        copy = pltpu.make_async_remote_copy(
+            src_ref=work.at[x],
+            dst_ref=work.at[x],
+            send_sem=q_send.at[t - 1],
+            recv_sem=q_recv.at[t - 1],
+            device_id=along_x(lax.rem(x + t, RING)),
+            device_id_type=pl.DeviceIdType.MESH,
+        )
+        copy.start()
+        quarters.append(copy)
+    for copy in quarters:
+        copy.wait()
+    for ring in (wide_x, wide_y, thin_x, thin_y):
+        ring.drain()
+    for copy in crossed + spread:
+        copy.wait_send()
+
+    whole[0] = work[...].reshape(whole.shape[1:])
+    invert(whole, range(1), 32, 16)
+    out[...] = whole[0, pl.ds(pl.multiple_of(x * rows, rows), rows), :]
 
 
 def shards(inner_pivots, lower_blocks, upper_blocks, separator_pivots, separator_ids, coupling_count):
@@ -103,6 +282,8 @@
     inverses = lax.all_gather(inner_inverse, "cols", axis=0, tiled=True)
 
     group = 6
+    spots = separators // CORES
+    schur_shape = (CORES, 2, 2, RING, spots, TILE, size)
     block = pl.BlockSpec((group, 1, size, size), lambda s, *_: (s, 0, 0, 0))
     lower_factor, schur = pl.pallas_call(
         functools.partial(couplings_kernel, group),
@@ -110,26 +291,47 @@
             num_scalar_prefetch=3,
             grid=(couplings // group,),
             in_specs=[pl.BlockSpec((group, size, size), lambda s, *_: (s, 0, 0)), block, block],
-            out_specs=[block, pl.BlockSpec((separators, size, size), lambda s, *_: (0, 0, 0))],
+            out_specs=[block, pl.BlockSpec(schur_shape, lambda s, *_: (0,) * len(schur_shape))],
         ),
         out_shape=[
             jax.ShapeDtypeStruct(lower_blocks.shape, f32),
-            jax.ShapeDtypeStruct((separators, size, size), f32),
+            jax.ShapeDtypeStruct(schur_shape, f32),
         ],
         compiler_params=params,
     )(col[None], separator_ids.reshape(-1), coupling_count, inverses, lower_blocks, upper_blocks)
 
-    summed = lax.psum_scatter(schur, "rows", scatter_dimension=0, tiled=True)
-    summed = lax.psum(summed, "cols")
-    pivots = lax.all_gather(separator_pivots, "cols", axis=1, tiled=True)
+    rows = separator_pivots.shape[1]
+    tile = (TILE, size)
     own = pl.pallas_call(
-        separator_kernel,
-        out_shape=jax.ShapeDtypeStruct(separator_pivots.shape[1:], f32),
-        in_specs=[VMEM, VMEM, SMEM],
+        separators_kernel,
+        out_shape=jax.ShapeDtypeStruct((rows, size), f32),
+        in_specs=[pl.BlockSpec(memory_space=pl.ANY), VMEM],
         out_specs=VMEM,
-        scratch_shapes=[pltpu.VMEM((1, size, size), f32)],
-        compiler_params=params,
-    )(pivots[0], summed[0], col[None])
+        scratch_shapes=[
+            pltpu.VMEM(schur_shape[1:], f32),
+            pltpu.VMEM(schur_shape[1:], f32),
+            pltpu.VMEM((6, spots) + tile, f32),
+            pltpu.VMEM((6, RING, DEPTH) + tile, f32),
+            pltpu.VMEM((2, spots) + tile, f32),
+            pltpu.VMEM((2, RING, DEPTH) + tile, f32),
+            pltpu.VMEM((6, DEPTH) + tile, f32),
+            pltpu.VMEM((6, DEPTH) + tile, f32),
+            pltpu.VMEM((DEPTH, 4) + tile, f32),
+            pltpu.VMEM((DEPTH - 1, 4) + tile, f32),
+            pltpu.VMEM((RING, rows, size), f32),
+            pltpu.VMEM((1, size, size), f32),
+            pltpu.SemaphoreType.DMA((4, 6)),
+            pltpu.SemaphoreType.DMA((4, 6)),
+            pltpu.SemaphoreType.DMA((4,)),
+            pltpu.SemaphoreType.DMA((4,)),
+            pltpu.SemaphoreType.DMA((4,)),
+            pltpu.SemaphoreType.DMA((DEPTH - 1,)),
+            pltpu.SemaphoreType.DMA((DEPTH - 1,)),
+            pltpu.SemaphoreType.DMA((RING - 1,)),
+            pltpu.SemaphoreType.DMA((RING - 1,)),
+        ],
+        compiler_params=pltpu.CompilerParams(vmem_limit_bytes=GRANT, collective_id=1, has_side_effects=True),
+    )(schur, separator_pivots[0])
     return inner_inverse, lower_factor, own[None]
 
 

time: 279 us -> 127 us (0.46)
  waiting for transfers between devices: 223 us -> 44.4 us
  Pallas kernels: 23.4 us -> 60.6 us
  blocking collectives: 12.1 us -> 0 us
    reduce_scatter x1 -> x0, waiting for transfers between devices: 145 us -> none  [shards(): summed = lax.psum_scatter(schur, 'rows', scatter_dimension=0, tiled=True)]
    pallas_call x1, Pallas kernels: 3.69 us -> 40.6 us  [shards(): pl.pallas_call(separators_kernel, out_shape=jax.ShapeDtypeStruct((rows, s...]
    psum x1 -> x0, waiting for transfers between devices: 33.3 us -> none  [shards(): summed = lax.psum(summed, 'cols')]
    all_gather x1 -> x0, blocking collectives: 12.1 us -> none  [shards(): pivots = lax.all_gather(separator_pivots, 'cols', axis=1, tiled=True)]
    unnamed x12 -> x13, local copies, waits for them, and re-layouts: 5.17 us -> 7.12 us
  transfers between devices with their start and end apart: 3 -> 1, of which waited for: 3 -> 1; matrix products, arithmetic and copies ran while one was open for 0% -> 0% of each run, Pallas kernels for 0% -> 0%
where the time goes in v1:
time: 127 us; the launch traced here: 126 us
  Pallas kernels  60.6 us (48%)
  waiting for transfers between devices  44.4 us (35%)
  between operations  14.1 us (11%)
  local copies, waits for them, and re-layouts  7.12 us (6%)
    all_gather x1, waiting for transfers between devices, shards(): inverses = lax.all_gather(inner_inverse, 'cols', axis=0, tiled=True)  44.4 us
    pallas_call x1, Pallas kernels, shards(): pl.pallas_call(separators_kernel, out_shape=jax.ShapeDtypeStruct((rows, s...  40.6 us
    pallas_call x1, Pallas kernels, shards(): pl.pallas_call(functools.partial(couplings_kernel, group), grid_spec=pltp...  10.8 us
    pallas_call x1, Pallas kernels, shards(): pl.pallas_call(interiors_kernel, out_shape=jax.ShapeDtypeStruct((count, s...  9.26 us
    unnamed x13, local copies, waits for them, and re-layouts  7.12 us
  transfers between devices with their start and end apart: 1, of which 1 were waited for; matrix products, arithmetic and copies ran while one was open for 0% of the time, Pallas kernels for 0%

profile of v1, /device:TPU:2, one launch (start us, length us, event | category | flops | bytes accessed | tf_op | source)
XLA Modules:
  0.0 126.3 jit_solution(394586359684503086)
XLA Ops:
  7.2 0.0 all-gather.2.cloned.1.call-start
  7.2 0.0 copy-start.2
  7.2 1.1 copy-done.2
  8.3 9.3 %shard_map.85 = f32[12,128,128]{2,1,0:T(8,128)} custom-call(f32[12,128,128]{2,1,0:T(8,128)S(1)} %copy-done.2), custom_call_target="tpu_custom_call" | custom-call | tf_op jit(solution)/shard_map/pallas_call | solution.py:275
  17.6 0.0 all-gather.2.cloned.1.call-update
  17.6 44.4 %all-gather.2.cloned.1.call-done.inverses = f32[48,128,128]{2,1,0:T(8,128)} async-done(((f32[12,128,128]{2,1,0:T(8,128)}), f32[48,128,128]{2,1,0:T(8,128)}) %all-gather.2.cloned.1.call-update) | async-done | bytes 3145744 | tf_op jit(solution)/shard_map/all_gather | solution.py:282
  62.0 0.0 copy-start.1
  62.0 1.9 %copy-done.1 = f32[48,128,128]{2,1,0:T(8,128)S(1)} copy-done((f32[48,128,128]{2,1,0:T(8,128)S(1)}, f32[48,128,128]{2,1,0:T(8,128)}, u32[]{:S(2)}) %copy-start.1) | copy-done | bytes 3145752
  63.9 0.0 copy-start.4
  63.9 0.7 copy-done.4
  64.6 0.0 copy-start.5
  64.6 0.7 copy-done.5
  65.2 0.0 copy-start.3
  65.2 10.8 %shard_map.86 = (f32[48,1,128,128]{3,2,1,0:T(8,128)}, f32[2,2,2,4,32,8,128]{6,5,4,3,2,1,0:T(8,128)}) custom-call(s32[1]{0:T(128)} %bitcast.first_slot, s32[48]{0:T(128)S(1)} %bitcast.6, s32[48]{0:T(128)S(1)} %copy-done.5, f32[48,128,128]{2,1,0:T(8,128)S(1)} %copy-done.1, f32[48,1,128,128]{3,2,1,0:T(8,128)} %lower.1, f32[48,1,128,128]{3,2,1,0:T(8,128)} %upper.1), custom_call_target="tpu_custom_call" | custom-call | tf_op jit(solution)/shard_map/pallas_call | solution.py:288
  76.0 0.0 copy-done.3
  76.0 0.0 copy-start
  76.0 2.2 %copy-done = f32[2,2,2,4,32,8,128]{6,5,4,3,2,1,0:T(8,128)S(1)} copy-done((f32[2,2,2,4,32,8,128]{6,5,4,3,2,1,0:T(8,128)S(1)}, f32[2,2,2,4,32,8,128]{6,5,4,3,2,1,0:T(8,128)}, u32[]{:S(2)}) %copy-start) | copy-done | bytes 4194328
  78.2 40.6 %shard_map.87 = f32[32,128]{1,0:T(8,128)S(1)} custom-call(f32[2,2,2,4,32,8,128]{6,5,4,3,2,1,0:T(8,128)S(1)} %copy-done, f32[32,128]{1,0:T(8,128)S(1)} %bitcast.5), custom_call_target="tpu_custom_call" | custom-call | tf_op jit(solution)/shard_map/pallas_call | solution.py:305
  118.8 0.6 copy.10
Async XLA Ops:
  7.2 54.9 %all-gather.2.cloned.1.call-start = ((), (), s32[]{:S(2)}) async-start(), calls=%async_computation | async-start | bytes 3932160 | tf_op jit(solution)/shard_map/all_gather | solution.py:282
  7.2 1.1 copy-start.2
  62.0 1.9 %copy-start.1 = (f32[48,128,128]{2,1,0:T(8,128)S(1)}, f32[48,128,128]{2,1,0:T(8,128)}, u32[]{:S(2)}) copy-start(f32[48,128,128]{2,1,0:T(8,128)} %all-gather.2.cloned.1.call-done.inverses) | copy-start | bytes 9437188
  63.9 0.7 copy-start.4
  64.6 0.7 copy-start.5
  65.2 10.8 %copy-start.3 = (f32[1,32,128]{2,1,0:T(8,128)S(1)}, f32[1,32,128]{2,1,0:T(8,128)}, u32[]{:S(2)}) copy-start(f32[1,32,128]{2,1,0:T(8,128)} %param.9) | copy-start | bytes 49156
  76.0 2.2 %copy-start = (f32[2,2,2,4,32,8,128]{6,5,4,3,2,1,0:T(8,128)S(1)}, f32[2,2,2,4,32,8,128]{6,5,4,3,2,1,0:T(8,128)}, u32[]{:S(2)}) copy-start(f32[2,2,2,4,32,8,128]{6,5,4,3,2,1,0:T(8,128)} %get-tuple-element.6.schur) | copy-start | bytes 12582916
Sparse Core Ops, SparseCore 0:
  17.8 44.2 all-gather.1

commit v2 on v1

--- a/solution.py
+++ b/solution.py
@@ -10,8 +10,9 @@
 HIGH = lax.Precision.HIGH
 VMEM = pl.BlockSpec(memory_space=pltpu.VMEM)
 SMEM = pl.BlockSpec(memory_space=pltpu.SMEM)
+ANY = pl.BlockSpec(memory_space=pl.ANY)
 GRANT = 48 << 20
-CORES, RING, DEPTH, TILE = 2, 4, 8, 8
+CORES, RING, DEPTH, TILE, GROUPS = 2, 4, 8, 8, 2
 
 
 def dot(a, b):
@@ -43,46 +44,50 @@
     return slabs
 
 
-def invert(ref, members, panel, ahead):
-    size = ref.shape[-1]
+def eliminate_by_tile(slabs, first):
+    depth, width = slabs[0].shape
+    lanes = lax.broadcasted_iota(jnp.int32, (1, width), 1)
+    rows = lax.broadcasted_iota(jnp.int32, (TILE, width), 0)
+    tiles = [[slab[t : t + TILE, :] for t in range(0, depth, TILE)] for slab in slabs]
+    for q in range(depth // TILE):
+        base = first + q * TILE
+        inside = (lanes >= base) & (lanes < base + TILE)
+        for parts in tiles:
+            spread = [
+                [jnp.broadcast_to(part[:, base + t : base + t + 1], (TILE, width)) for t in range(TILE)]
+                for part in parts
+            ]
+            pivot, columns = parts[q], spread[q]
+            for t in range(TILE):
+                at_lane = (lanes == base + t).astype(jnp.float32)
+                at_row = (rows == t).astype(jnp.float32)
+                inverse = 1.0 / columns[t][t : t + 1, :]
+                pivot_row = (pivot[t : t + 1, :] + at_lane) * inverse
+                column = columns[t] - at_row
+                for u in range(t + 1, TILE):
+                    columns[u] = columns[u] - column * (columns[u][t : t + 1, :] * inverse)
+                pivot = pivot - column * pivot_row
+            parts[q] = pivot
+            for other in range(len(parts)):
+                if other != q:
+                    value = jnp.where(inside, 0.0, parts[other])
+                    for t in range(TILE):
+                        value = value - spread[other][t] * pivot[t : t + 1, :]
+                    parts[other] = value
+    return [jnp.concatenate(parts, axis=0) for parts in tiles]
+
+
+def invert(refs, panel, eliminate_slabs):
+    size = refs[0].shape[-1]
     lanes = lax.broadcasted_iota(jnp.int32, (1, size), 1)
     for first in range(0, size, panel):
-        slabs = eliminate([ref[b, first : first + panel, :] for b in members], first, ahead)
+        slabs = eliminate_slabs([ref[first : first + panel, :] for ref in refs], first)
         inside = (lanes >= first) & (lanes < first + panel)
-        for b, slab in zip(members, slabs):
-            whole = ref[b]
+        for ref, slab in zip(refs, slabs):
+            whole = ref[...]
             update = dot(whole[:, first : first + panel], slab)
-            ref[b] = jnp.where(inside, 0.0, whole) - update
-            ref[b, first : first + panel, :] = slab
-
-
-def interiors_kernel(pivots, out):
-    out[...] = pivots[...]
-    invert(out, range(pivots.shape[0]), 8, 8)
-
-
-def couplings_kernel(group, first_slot, ids, counts, inverses, lower, upper, factor, schur):
-    step = pl.program_id(0)
-
-    @pl.when(step == 0)
-    def _():
-        schur[...] = jnp.zeros_like(schur)
-
-    products = []
-    for g in range(group):
-        live = first_slot[0] < counts[step * group + g]
-        value = jnp.where(live, dot(lower[g, 0], inverses[g]), 0.0)
-        factor[g, 0] = value
-        products.append(dot(value, upper[g, 0]))
-    for g in range(group):
-        j = ids[step * group + g]
-        core, spot = lax.rem(j, CORES), lax.div(j, CORES)
-        for quarter in range(RING):
-            for half in range(2):
-                for way in range(2):
-                    row = quarter * 32 + half * 16 + way * TILE
-                    at = (core, half, way, quarter, spot)
-                    schur[at] = schur[at] + products[g][row : row + TILE, :]
+            ref[...] = jnp.where(inside, 0.0, whole) - update
+            ref[first : first + panel, :] = slab
 
 
 class Ring:
@@ -136,14 +141,21 @@
             copy.wait_send()
 
 
-def separators_kernel(
-    schur, pivots, out, mine, other, x_wide, y_wide, x_part, y_part, x_thin, y_thin, stack, column, work, whole,
-    send, recv, load, core_send, core_recv, z_send, z_recv, q_send, q_recv,
+def kernel(
+    ids, ids_row, counts, pivots, lower, upper, own_pivots, inner, factor, out,
+    inverses, low, up, fac, chain, link, theirs, mine, other, x_wide, y_wide, x_part, y_part, x_thin, y_thin,
+    stack, column, work, whole,
+    pivot_load, block_load, gather_send, gather_recv, inner_store, factor_store,
+    send, recv, core_send, core_recv, z_send, z_recv, q_send, q_recv,
 ):
     row, x = lax.axis_index("rows"), lax.axis_index("cols")
     core = lax.rem(row, CORES)
     z = lax.rem(lax.div(row, CORES), DEPTH)
     y = lax.div(row, CORES * DEPTH)
+    count, size = pivots.shape[0], pivots.shape[-1]
+    couplings, separators = counts.shape[0], 2 * theirs.shape[3]
+    group = count // GROUPS
+    part = group // 2
 
     def device(x_at, y_at, z_at, core_at):
         return {"rows": (y_at * DEPTH + z_at) * CORES + core_at, "cols": x_at}
@@ -161,31 +173,156 @@
     for peer in greeted:
         pl.semaphore_signal(barrier, inc=1, device_id=peer, device_id_type=pl.DeviceIdType.MESH)
 
-    loads = []
-    for part in range(4):
-        half, way = part // 2, part % 2
-        copy = pltpu.make_async_copy(schur.at[core, half, way], mine.at[half, way], load.at[part])
+    def source(offset):
+        return lax.rem(x + offset, RING)
+
+    def load_pivots(g):
+        members = pl.ds(g * group, group)
+        return pltpu.make_async_copy(pivots.at[members], inverses.at[x, members], pivot_load.at[g])
+
+    def load_blocks(offset):
+        members = pl.ds(source(offset) * count, count)
+        return (
+            pltpu.make_async_copy(lower.at[members, 0], low.at[members], block_load.at[0, offset]),
+            pltpu.make_async_copy(upper.at[members, 0], up.at[members], block_load.at[1, offset]),
+        )
+
+    for g in range(GROUPS):
+        load_pivots(g).start()
+    for offset in range(RING):
+        for copy in load_blocks(offset):
+            copy.start()
+    pl.semaphore_wait(barrier, len(greeted))
+
+    def gather(kind, g):
+        block = inverses.at[x, pl.ds(g * group, group)]
+        if kind == 2:
+            block = inverses.at[source(3), pl.ds(g * group, part)]
+        if kind == 3:
+            block = inverses.at[source(1), pl.ds(g * group + part, part)]
+        return pltpu.make_async_remote_copy(
+            src_ref=block,
+            dst_ref=block,
+            send_sem=gather_send.at[kind, g],
+            recv_sem=gather_recv.at[kind, g],
+            device_id=along_x(source(1 if kind % 2 == 0 else 3)),
+            device_id_type=pl.DeviceIdType.MESH,
+        )
+
+    def make_inverses(g, carry):
+        load_pivots(g).wait()
+        invert([inverses.at[x, g * group + b] for b in range(group)], 16, eliminate_by_tile)
+        gather(0, g).start()
+        gather(1, g).start()
+        return carry
+
+    lax.fori_loop(0, GROUPS, make_inverses, 0)
+    store_inner = pltpu.make_async_copy(inverses.at[x], inner, inner_store)
+    store_inner.start()
+
+    lane = lax.broadcasted_iota(jnp.int32, (1, couplings), 1)
+    owner, local = lax.div(lane, count), lax.rem(lane, count)
+    behind = lax.rem(owner + RING - x, RING)
+    turn = jnp.where(behind == 3, 0, jnp.where(behind == 1, group, 2 * group))
+    later = count + lax.div(local, group) * 3 * group + turn + lax.rem(local, group)
+    place = jnp.where(behind == 0, local, later)
+    named = ids_row[...]
+
+    def newest(target, limit):
+        found = jnp.max(jnp.where((named == target) & (place < limit), place, -1))
+        return jnp.where(found < 0, couplings, found)
+
+    def interior(n):
+        late = n - count
+        third = lax.div(lax.rem(late, 3 * group), group)
+        offset = jnp.where(third == 0, 3, jnp.where(third == 1, 1, 2))
+        in_own = lax.div(late, 3 * group) * group + lax.rem(late, group)
+        return jnp.where(n < count, x * count + n, source(offset) * count + in_own)
+
+    def find_previous(n, carry):
+        link[n] = newest(ids[interior(n)], n)
+        return carry
+
+    def find_last(j, carry):
+        link[couplings + j] = newest(j, couplings)
+        return carry
+
+    lax.fori_loop(0, couplings, find_previous, 0, unroll=8)
+    lax.fori_loop(0, separators, find_last, 0, unroll=8)
+    chain[couplings] = jnp.zeros((size, size), jnp.float32)
+
+    stores = []
+
+    def couple(offset, first, length, place_first):
+        base = source(offset) * count + first
+        for b in range(length):
+            i, n = base + b, place_first + b
+            value = jnp.where(x < counts[i], dot(low[i], inverses[source(offset), first + b]), 0.0)
+            fac[i] = value
+            chain[n] = dot(value, up[i]) + chain[link[n]]
+        members = pl.ds(base, length)
+        copy = pltpu.make_async_copy(fac.at[members], factor.at[members, 0], factor_store.at[len(stores)])
         copy.start()
-        loads.append(copy)
-    pl.semaphore_wait(barrier, len(greeted))
+        stores.append(copy)
+
+    def await_blocks(offset):
+        for copy in load_blocks(offset):
+            copy.wait()
+
+    await_blocks(0)
+    gather(0, 0).wait_recv()
+    gather(2, 0).start()
+    gather(1, 0).wait_recv()
+    gather(3, 0).start()
+    for g in range(GROUPS):
+        couple(0, g * group, group, g * group)
+    for offset in (3, 1, 2):
+        await_blocks(offset)
+    for g in range(GROUPS):
+        place_first = count + g * 3 * group
+        if g > 0:
+            gather(0, g).wait_recv()
+            gather(2, g).start()
+            gather(1, g).wait_recv()
+            gather(3, g).start()
+        couple(3, g * group, group, place_first)
+        couple(1, g * group, group, place_first + group)
+        gather(2, g).wait_recv()
+        couple(2, g * group, part, place_first + 2 * group)
+        gather(3, g).wait_recv()
+        couple(2, g * group + part, part, place_first + 2 * group + part)
+
+    def lay_out(parity, into):
+        def body(spot, carry):
+            value = chain[link[couplings + spot * CORES + parity]]
+            for quarter in range(RING):
+                for half in range(2):
+                    for way in range(2):
+                        at = quarter * 32 + half * 16 + way * TILE
+                        into[half, way, quarter, spot] = value[at : at + TILE, :]
+            return carry
+
+        lax.fori_loop(0, separators // CORES, body, 0, unroll=4)
+
+    lay_out(1 - core, theirs)
 
     crossed = []
-    for part in range(4):
-        half, way = part // 2, part % 2
+    for piece in range(4):
+        half, way = piece // 2, piece % 2
         copy = pltpu.make_async_remote_copy(
-            src_ref=schur.at[1 - core, half, way],
+            src_ref=theirs.at[half, way],
             dst_ref=other.at[half, way],
-            send_sem=core_send.at[part],
-            recv_sem=core_recv.at[part],
+            send_sem=core_send.at[piece],
+            recv_sem=core_recv.at[piece],
             device_id=sibling,
             device_id_type=pl.DeviceIdType.MESH,
         )
         copy.start()
         crossed.append(copy)
-    for part in range(4):
-        half, way = part // 2, part % 2
-        loads[part].wait()
-        crossed[part].wait_recv()
+    lay_out(core, mine)
+    for piece in range(4):
+        half, way = piece // 2, piece % 2
+        crossed[piece].wait_recv()
         mine[half, way] = mine[half, way] + other[half, way]
 
     def keep_x(way, value):
@@ -238,8 +375,8 @@
         spread[t - 1].wait_recv()
         total = total + column[t - 1]
 
-    rows = pivots.shape[0]
-    work[x] = pivots[...] - total.reshape(rows, total.shape[-1])
+    rows = own_pivots.shape[0]
+    work[x] = own_pivots[...] - total.reshape(rows, total.shape[-1])
     quarters = []
     for t in range(1, RING):
         copy = pltpu.make_async_remote_copy(
@@ -259,79 +396,81 @@
     for copy in crossed + spread:
         copy.wait_send()
 
-    whole[0] = work[...].reshape(whole.shape[1:])
-    invert(whole, range(1), 32, 16)
-    out[...] = whole[0, pl.ds(pl.multiple_of(x * rows, rows), rows), :]
+    whole[...] = work[...].reshape(whole.shape)
+    invert([whole], 32, functools.partial(eliminate, ahead=16))
+    out[...] = whole[pl.ds(pl.multiple_of(x * rows, rows), rows), :]
+    for g in range(GROUPS):
+        for kind in range(4):
+            gather(kind, g).wait_send()
+    for copy in stores + [store_inner]:
+        copy.wait()
 
 
 def shards(inner_pivots, lower_blocks, upper_blocks, separator_pivots, separator_ids, coupling_count):
     f32 = jnp.float32
     count, size = inner_pivots.shape[0], inner_pivots.shape[1]
     couplings = lower_blocks.shape[0]
-    col = lax.axis_index("cols").astype(jnp.int32)
     separators = separator_pivots.shape[0] * lax.axis_size("rows")
-    params = pltpu.CompilerParams(vmem_limit_bytes=GRANT)
-
-    inner_inverse = pl.pallas_call(
-        interiors_kernel,
-        out_shape=jax.ShapeDtypeStruct((count, size, size), f32),
-        in_specs=[VMEM],
-        out_specs=VMEM,
-        compiler_params=params,
-    )(inner_pivots)
-    inverses = lax.all_gather(inner_inverse, "cols", axis=0, tiled=True)
-
-    group = 6
+    rows = separator_pivots.shape[1]
     spots = separators // CORES
-    schur_shape = (CORES, 2, 2, RING, spots, TILE, size)
-    block = pl.BlockSpec((group, 1, size, size), lambda s, *_: (s, 0, 0, 0))
-    lower_factor, schur = pl.pallas_call(
-        functools.partial(couplings_kernel, group),
-        grid_spec=pltpu.PrefetchScalarGridSpec(
-            num_scalar_prefetch=3,
-            grid=(couplings // group,),
-            in_specs=[pl.BlockSpec((group, size, size), lambda s, *_: (s, 0, 0)), block, block],
-            out_specs=[block, pl.BlockSpec(schur_shape, lambda s, *_: (0,) * len(schur_shape))],
-        ),
+    tile = (TILE, size)
+    block = (size, size)
+    dma = pltpu.SemaphoreType.DMA
+    vmem = lambda *shape: pltpu.VMEM(shape, f32)
+    inner_inverse, lower_factor, own = pl.pallas_call(
+        kernel,
         out_shape=[
+            jax.ShapeDtypeStruct(inner_pivots.shape, f32),
             jax.ShapeDtypeStruct(lower_blocks.shape, f32),
-            jax.ShapeDtypeStruct(schur_shape, f32),
+            jax.ShapeDtypeStruct((rows, size), f32),
         ],
-        compiler_params=params,
-    )(col[None], separator_ids.reshape(-1), coupling_count, inverses, lower_blocks, upper_blocks)
-
-    rows = separator_pivots.shape[1]
-    tile = (TILE, size)
-    own = pl.pallas_call(
-        separators_kernel,
-        out_shape=jax.ShapeDtypeStruct((rows, size), f32),
-        in_specs=[pl.BlockSpec(memory_space=pl.ANY), VMEM],
-        out_specs=VMEM,
+        in_specs=[SMEM, VMEM, SMEM, ANY, ANY, ANY, VMEM],
+        out_specs=[ANY, ANY, VMEM],
         scratch_shapes=[
-            pltpu.VMEM(schur_shape[1:], f32),
-            pltpu.VMEM(schur_shape[1:], f32),
-            pltpu.VMEM((6, spots) + tile, f32),
-            pltpu.VMEM((6, RING, DEPTH) + tile, f32),
-            pltpu.VMEM((2, spots) + tile, f32),
-            pltpu.VMEM((2, RING, DEPTH) + tile, f32),
-            pltpu.VMEM((6, DEPTH) + tile, f32),
-            pltpu.VMEM((6, DEPTH) + tile, f32),
-            pltpu.VMEM((DEPTH, 4) + tile, f32),
-            pltpu.VMEM((DEPTH - 1, 4) + tile, f32),
-            pltpu.VMEM((RING, rows, size), f32),
-            pltpu.VMEM((1, size, size), f32),
-            pltpu.SemaphoreType.DMA((4, 6)),
-            pltpu.SemaphoreType.DMA((4, 6)),
-            pltpu.SemaphoreType.DMA((4,)),
-            pltpu.SemaphoreType.DMA((4,)),
-            pltpu.SemaphoreType.DMA((4,)),
-            pltpu.SemaphoreType.DMA((DEPTH - 1,)),
-            pltpu.SemaphoreType.DMA((DEPTH - 1,)),
-            pltpu.SemaphoreType.DMA((RING - 1,)),
-            pltpu.SemaphoreType.DMA((RING - 1,)),
+            vmem(RING, count, *block),
+            vmem(couplings, *block),
+            vmem(couplings, *block),
+            vmem(couplings, *block),
+            vmem(couplings + 1, *block),
+            pltpu.SMEM((couplings + separators,), jnp.int32),
+            vmem(2, 2, RING, spots, *tile),
+            vmem(2, 2, RING, spots, *tile),
+            vmem(2, 2, RING, spots, *tile),
+            vmem(6, spots, *tile),
+            vmem(6, RING, DEPTH, *tile),
+            vmem(2, spots, *tile),
+            vmem(2, RING, DEPTH, *tile),
+            vmem(6, DEPTH, *tile),
+            vmem(6, DEPTH, *tile),
+            vmem(DEPTH, 4, *tile),
+            vmem(DEPTH - 1, 4, *tile),
+            vmem(RING, rows, size),
+            vmem(*block),
+            dma((GROUPS,)),
+            dma((2, RING)),
+            dma((4, GROUPS)),
+            dma((4, GROUPS)),
+            dma,
+            dma((5 * GROUPS,)),
+            dma((4, 6)),
+            dma((4, 6)),
+            dma((4,)),
+            dma((4,)),
+            dma((DEPTH - 1,)),
+            dma((DEPTH - 1,)),
+            dma((RING - 1,)),
+            dma((RING - 1,)),
         ],
-        compiler_params=pltpu.CompilerParams(vmem_limit_bytes=GRANT, collective_id=1, has_side_effects=True),
-    )(schur, separator_pivots[0])
+        compiler_params=pltpu.CompilerParams(vmem_limit_bytes=GRANT, collective_id=0, has_side_effects=True),
+    )(
+        separator_ids.reshape(-1),
+        separator_ids.reshape(1, -1),
+        coupling_count,
+        inner_pivots,
+        lower_blocks,
+        upper_blocks,
+        separator_pivots[0],
+    )
     return inner_inverse, lower_factor, own[None]
 
 

time: 127 us -> 85.1 us (0.67)
  waiting for transfers between devices: 44.4 us -> 0 us
  Pallas kernels: 60.6 us -> 78 us
  between operations: 14.1 us -> 0.65 us
    all_gather x1 -> x0, waiting for transfers between devices: 44.4 us -> none  [shards(): inverses = lax.all_gather(inner_inverse, 'cols', axis=0, tiled=True)]
    pallas_call x3 -> x1, Pallas kernels: 60.6 us -> 78 us  [shards(): pl.pallas_call(kernel, out_shape=[jax.ShapeDtypeStruct(inner_pivots.shape...]
    unnamed x13 -> x11, local copies, waits for them, and re-layouts: 7.12 us -> 6.3 us
  transfers between devices with their start and end apart: 1 -> 0, of which waited for: 1 -> 0; matrix products, arithmetic and copies ran while one was open for 0% -> 0% of each run, Pallas kernels for 0% -> 0%
where the time goes in v2:
time: 85.1 us; the launch traced here: 84.9 us
  Pallas kernels  78 us (92%)
  local copies, waits for them, and re-layouts  6.3 us (7%)
    pallas_call x1, Pallas kernels, shards(): pl.pallas_call(kernel, out_shape=[jax.ShapeDtypeStruct(inner_pivots.shape...  78 us
    unnamed x11, local copies, waits for them, and re-layouts  6.3 us

profile of v2, /device:TPU:2, one launch (start us, length us, event | category | flops | bytes accessed | tf_op | source)
XLA Modules:
  0.0 84.9 jit_solution(17979769861069614997)
XLA Ops:
  0.6 0.0 copy-start
  0.6 1.1 %copy-done = f32[12,128,128]{2,1,0:T(8,128)S(1)} copy-done((f32[12,128,128]{2,1,0:T(8,128)S(1)}, f32[12,128,128]{2,1,0:T(8,128)}, u32[]{:S(2)}) %copy-start) | copy-done | bytes 786456
  1.8 0.0 copy-start.1
  1.8 0.7 copy-done.1
  2.5 0.0 copy-start.2
  2.5 0.7 copy-done.2
  3.1 0.0 copy-start.3
  3.1 0.7 copy-done.3
  3.8 78.0 %shard_map.85 = (f32[12,128,128]{2,1,0:T(8,128)S(1)}, f32[48,1,128,128]{3,2,1,0:T(8,128)S(1)}, f32[32,128]{1,0:T(8,128)S(1)}) custom-call(s32[48]{0:T(128)S(1)} %bitcast.6, s32[1,48]{1,0:T(1,128)S(1)} %bitcast.7, s32[48]{0:T(128)S(1)} %copy-done.3, f32[12,128,128]{2,1,0:T(8,128)S(1)} %copy-done, f32[48,1,128,128]{3,2,1,0:T(8,128)} %lower.1, ...), custom_call_target="tpu_custom_call" | custom-call | tf_op jit(solution)/shard_map/pallas_call | solution.py:420
  81.8 0.9 %copy.12 = f32[12,128,128]{2,1,0:T(8,128)} copy(f32[12,128,128]{2,1,0:T(8,128)S(1)} %get-tuple-element.12) | data formatting | bytes 1572864
  82.7 1.7 %copy.13 = f32[48,1,128,128]{3,2,1,0:T(8,128)} copy(f32[48,1,128,128]{3,2,1,0:T(8,128)S(1)} %get-tuple-element.13) | data formatting | bytes 6291456
  84.3 0.6 copy.14
Async XLA Ops:
  0.6 1.1 %copy-start = (f32[12,128,128]{2,1,0:T(8,128)S(1)}, f32[12,128,128]{2,1,0:T(8,128)}, u32[]{:S(2)}) copy-start(f32[12,128,128]{2,1,0:T(8,128)} %pivots.1) | copy-start | bytes 2359300
  1.8 0.7 copy-start.1
  2.5 0.7 copy-start.2
  3.1 0.7 copy-start.3

commit v3 on v2

--- a/solution.py
+++ b/solution.py
@@ -9,10 +9,10 @@
 
 HIGH = lax.Precision.HIGH
 VMEM = pl.BlockSpec(memory_space=pltpu.VMEM)
-SMEM = pl.BlockSpec(memory_space=pltpu.SMEM)
+HBM = pl.BlockSpec(memory_space=pltpu.HBM)
 ANY = pl.BlockSpec(memory_space=pl.ANY)
-GRANT = 48 << 20
-CORES, RING, DEPTH, TILE, GROUPS = 2, 4, 8, 8, 2
+GRANT = 63 << 20
+CORES, RING, DEPTH, TILE = 2, 4, 8, 8
 
 
 def dot(a, b):
@@ -77,7 +77,7 @@
     return [jnp.concatenate(parts, axis=0) for parts in tiles]
 
 
-def invert(refs, panel, eliminate_slabs):
+def invert(refs, panel, eliminate_slabs, after_first=None):
     size = refs[0].shape[-1]
     lanes = lax.broadcasted_iota(jnp.int32, (1, size), 1)
     for first in range(0, size, panel):
@@ -88,6 +88,8 @@
             update = dot(whole[:, first : first + panel], slab)
             ref[...] = jnp.where(inside, 0.0, whole) - update
             ref[first : first + panel, :] = slab
+        if first == 0 and after_first is not None:
+            after_first()
 
 
 class Ring:
@@ -141,21 +143,30 @@
             copy.wait_send()
 
 
+RAW = 2
+PARTS = 4
+PIECES = ((0, RAW), (RAW, 6), (RAW + 6, 4))
+BLOCKS = (
+    (0, 0, 12), (3, 0, 2), (1, 0, 2), (2, 0, 2), (3, 2, 6), (1, 2, 6), (3, 8, 4), (1, 8, 4), (2, 2, 6), (2, 8, 4),
+)
+PLACES = tuple(sum(block[2] for block in BLOCKS[:k]) for k in range(len(BLOCKS)))
+
+
 def kernel(
-    ids, ids_row, counts, pivots, lower, upper, own_pivots, inner, factor, out,
-    inverses, low, up, fac, chain, link, theirs, mine, other, x_wide, y_wide, x_part, y_part, x_thin, y_thin,
-    stack, column, work, whole,
-    pivot_load, block_load, gather_send, gather_recv, inner_store, factor_store,
-    send, recv, core_send, core_recv, z_send, z_recv, q_send, q_recv,
+    ids_hbm, row_hbm, counts_hbm, pivots, lower, upper, own_hbm, inner, factor, out,
+    ids, ids_row, twin_row, counts, own_pivots,
+    inverses, low, up, fac, chain, twin, link, mine, x_wide, y_wide, x_part, y_part, x_thin, y_thin,
+    stack, column, work, bench,
+    small_load, pivot_load, block_load, gather_send, gather_recv, inner_store, factor_store,
+    twin_send, twin_recv, row_send, row_recv, send, recv, z_send, z_recv, q_send, q_recv,
 ):
     row, x = lax.axis_index("rows"), lax.axis_index("cols")
     core = lax.rem(row, CORES)
     z = lax.rem(lax.div(row, CORES), DEPTH)
     y = lax.div(row, CORES * DEPTH)
     count, size = pivots.shape[0], pivots.shape[-1]
-    couplings, separators = counts.shape[0], 2 * theirs.shape[3]
-    group = count // GROUPS
-    part = group // 2
+    couplings, spots = counts.shape[0], mine.shape[3]
+    group = PIECES[1][1]
 
     def device(x_at, y_at, z_at, core_at):
         return {"rows": (y_at * DEPTH + z_at) * CORES + core_at, "cols": x_at}
@@ -176,9 +187,12 @@
     def source(offset):
         return lax.rem(x + offset, RING)
 
-    def load_pivots(g):
-        members = pl.ds(g * group, group)
-        return pltpu.make_async_copy(pivots.at[members], inverses.at[x, members], pivot_load.at[g])
+    small = [
+        pltpu.make_async_copy(source_ref, into, small_load.at[k])
+        for k, (source_ref, into) in enumerate(
+            ((ids_hbm, ids), (row_hbm, ids_row), (counts_hbm, counts), (own_hbm, own_pivots))
+        )
+    ]
 
     def load_blocks(offset):
         members = pl.ds(source(offset) * count, count)
@@ -187,143 +201,159 @@
             pltpu.make_async_copy(upper.at[members, 0], up.at[members], block_load.at[1, offset]),
         )
 
-    for g in range(GROUPS):
-        load_pivots(g).start()
+    load_pivots = pltpu.make_async_copy(pivots, inverses.at[x], pivot_load)
+    load_pivots.start()
+    for copy in small:
+        copy.start()
+    pl.semaphore_wait(barrier, len(greeted))
+
+    def gather(kind, piece):
+        first, length = PIECES[piece]
+        first, length = ((first, length), (first, length), (first, length // 2), (first + length // 2, length // 2))[kind]
+        block = inverses.at[source((0, 0, 3, 1)[kind]), pl.ds(first, length)]
+        return pltpu.make_async_remote_copy(
+            src_ref=block,
+            dst_ref=block,
+            send_sem=gather_send.at[kind, piece],
+            recv_sem=gather_recv.at[kind, piece],
+            device_id=along_x(source(1 if kind % 2 == 0 else 3)),
+            device_id_type=pl.DeviceIdType.MESH,
+        )
+
+    def pass_on(piece):
+        for kind in (0, 1):
+            gather(kind, piece).wait_recv()
+            gather(kind + 2, piece).start()
+
+    load_pivots.wait()
+    gather(0, 0).start()
+    gather(1, 0).start()
     for offset in range(RING):
         for copy in load_blocks(offset):
             copy.start()
-    pl.semaphore_wait(barrier, len(greeted))
-
-    def gather(kind, g):
-        block = inverses.at[x, pl.ds(g * group, group)]
-        if kind == 2:
-            block = inverses.at[source(3), pl.ds(g * group, part)]
-        if kind == 3:
-            block = inverses.at[source(1), pl.ds(g * group + part, part)]
-        return pltpu.make_async_remote_copy(
-            src_ref=block,
-            dst_ref=block,
-            send_sem=gather_send.at[kind, g],
-            recv_sem=gather_recv.at[kind, g],
-            device_id=along_x(source(1 if kind % 2 == 0 else 3)),
-            device_id_type=pl.DeviceIdType.MESH,
-        )
+    send_row = pltpu.make_async_remote_copy(
+        src_ref=row_hbm, dst_ref=twin_row, send_sem=row_send, recv_sem=row_recv,
+        device_id=sibling, device_id_type=pl.DeviceIdType.MESH,
+    )
+    send_row.start()
 
     def make_inverses(g, carry):
-        load_pivots(g).wait()
-        invert([inverses.at[x, g * group + b] for b in range(group)], 16, eliminate_by_tile)
-        gather(0, g).start()
-        gather(1, g).start()
+        @pl.when(g == 1)
+        def _():
+            for kind in (0, 1):
+                gather(kind, 0).wait_send()
+
+        @pl.when(g == 2)
+        def _():
+            for kind in (2, 3):
+                gather(kind, 0).wait_recv()
+                gather(kind, 0).wait_send()
+
+        spots_of = []
+        for b in range(group):
+            at = source(jnp.where(g == 2, (3, 1, 2)[b % 3], 0))
+            spots_of.append((at, jnp.where(g == 2, b // 3, lax.rem(RAW + g * group + b, count))))
+            bench[b] = inverses[spots_of[b]]
+        invert([bench.at[b] for b in range(group)], 16, eliminate_by_tile)
+        for b in range(group):
+            inverses[spots_of[b]] = bench[b]
+
+        @pl.when(g == 0)
+        def _():
+            pass_on(0)
+            gather(0, 1).start()
+            gather(1, 1).start()
+
+        @pl.when(g == 1)
+        def _():
+            gather(0, 2).start()
+            gather(1, 2).start()
+
         return carry
 
-    lax.fori_loop(0, GROUPS, make_inverses, 0)
+    lax.fori_loop(0, 3, make_inverses, 0)
     store_inner = pltpu.make_async_copy(inverses.at[x], inner, inner_store)
     store_inner.start()
+    pass_on(1)
+    for copy in small:
+        copy.wait()
+    send_row.wait_recv()
 
     lane = lax.broadcasted_iota(jnp.int32, (1, couplings), 1)
     owner, local = lax.div(lane, count), lax.rem(lane, count)
     behind = lax.rem(owner + RING - x, RING)
-    turn = jnp.where(behind == 3, 0, jnp.where(behind == 1, group, 2 * group))
-    later = count + lax.div(local, group) * 3 * group + turn + lax.rem(local, group)
-    place = jnp.where(behind == 0, local, later)
-    named = ids_row[...]
-
-    def newest(target, limit):
+    place = jnp.zeros_like(lane)
+    for (offset, first, length), place_first in zip(BLOCKS, PLACES):
+        here = (behind == offset) & (local >= first) & (local < first + length)
+        place = jnp.where(here, local + (place_first - first), place)
+
+    def newest(named, target, limit):
         found = jnp.max(jnp.where((named == target) & (place < limit), place, -1))
         return jnp.where(found < 0, couplings, found)
 
-    def interior(n):
-        late = n - count
-        third = lax.div(lax.rem(late, 3 * group), group)
-        offset = jnp.where(third == 0, 3, jnp.where(third == 1, 1, 2))
-        in_own = lax.div(late, 3 * group) * group + lax.rem(late, group)
-        return jnp.where(n < count, x * count + n, source(offset) * count + in_own)
-
-    def find_previous(n, carry):
-        link[n] = newest(ids[interior(n)], n)
+    names, twin_names = ids_row[...], twin_row[...]
+    for (offset, first, length), place_first in zip(BLOCKS, PLACES):
+        for b in range(length):
+            link[place_first + b] = newest(names, ids[source(offset) * count + first + b], place_first + b)
+
+    def find_last(spot, carry):
+        link[couplings + spot] = newest(names, spot * CORES + core, couplings)
+        link[couplings + spots + spot] = newest(twin_names, spot * CORES + core, couplings)
         return carry
 
-    def find_last(j, carry):
-        link[couplings + j] = newest(j, couplings)
-        return carry
-
-    lax.fori_loop(0, couplings, find_previous, 0, unroll=8)
-    lax.fori_loop(0, separators, find_last, 0, unroll=8)
+    lax.fori_loop(0, spots, find_last, 0, unroll=8)
     chain[couplings] = jnp.zeros((size, size), jnp.float32)
+    twin[couplings] = jnp.zeros((size, size), jnp.float32)
 
     stores = []
 
-    def couple(offset, first, length, place_first):
-        base = source(offset) * count + first
+    crossed = []
+
+    def couple(block):
+        offset, first, length = BLOCKS[block]
+        base, place_first = source(offset) * count + first, PLACES[block]
         for b in range(length):
             i, n = base + b, place_first + b
             value = jnp.where(x < counts[i], dot(low[i], inverses[source(offset), first + b]), 0.0)
             fac[i] = value
             chain[n] = dot(value, up[i]) + chain[link[n]]
-        members = pl.ds(base, length)
-        copy = pltpu.make_async_copy(fac.at[members], factor.at[members, 0], factor_store.at[len(stores)])
+        members, places = pl.ds(base, length), pl.ds(place_first, length)
+        copy = pltpu.make_async_copy(fac.at[members], factor.at[members, 0], factor_store.at[block])
         copy.start()
         stores.append(copy)
-
-    def await_blocks(offset):
+        copy = pltpu.make_async_remote_copy(
+            src_ref=chain.at[places], dst_ref=twin.at[places],
+            send_sem=twin_send.at[block], recv_sem=twin_recv.at[block],
+            device_id=sibling, device_id_type=pl.DeviceIdType.MESH,
+        )
+        copy.start()
+        crossed.append(copy)
+
+    for offset in range(RING):
         for copy in load_blocks(offset):
             copy.wait()
-
-    await_blocks(0)
-    gather(0, 0).wait_recv()
-    gather(2, 0).start()
-    gather(1, 0).wait_recv()
-    gather(3, 0).start()
-    for g in range(GROUPS):
-        couple(0, g * group, group, g * group)
-    for offset in (3, 1, 2):
-        await_blocks(offset)
-    for g in range(GROUPS):
-        place_first = count + g * 3 * group
-        if g > 0:
-            gather(0, g).wait_recv()
-            gather(2, g).start()
-            gather(1, g).wait_recv()
-            gather(3, g).start()
-        couple(3, g * group, group, place_first)
-        couple(1, g * group, group, place_first + group)
-        gather(2, g).wait_recv()
-        couple(2, g * group, part, place_first + 2 * group)
-        gather(3, g).wait_recv()
-        couple(2, g * group + part, part, place_first + 2 * group + part)
-
-    def lay_out(parity, into):
-        def body(spot, carry):
-            value = chain[link[couplings + spot * CORES + parity]]
-            for quarter in range(RING):
-                for half in range(2):
-                    for way in range(2):
-                        at = quarter * 32 + half * 16 + way * TILE
-                        into[half, way, quarter, spot] = value[at : at + TILE, :]
-            return carry
-
-        lax.fori_loop(0, separators // CORES, body, 0, unroll=4)
-
-    lay_out(1 - core, theirs)
-
-    crossed = []
-    for piece in range(4):
-        half, way = piece // 2, piece % 2
-        copy = pltpu.make_async_remote_copy(
-            src_ref=theirs.at[half, way],
-            dst_ref=other.at[half, way],
-            send_sem=core_send.at[piece],
-            recv_sem=core_recv.at[piece],
-            device_id=sibling,
-            device_id_type=pl.DeviceIdType.MESH,
-        )
-        copy.start()
-        crossed.append(copy)
-    lay_out(core, mine)
-    for piece in range(4):
-        half, way = piece // 2, piece % 2
-        crossed[piece].wait_recv()
-        mine[half, way] = mine[half, way] + other[half, way]
+    for block in range(6):
+        couple(block)
+    pass_on(2)
+    couple(6)
+    couple(7)
+    for block, piece in ((8, 1), (9, 2)):
+        gather(2, piece).wait_recv()
+        gather(3, piece).wait_recv()
+        couple(block)
+    for copy in crossed:
+        copy.wait_recv()
+
+    def lay_out(spot, carry):
+        value = chain[link[couplings + spot]] + twin[link[couplings + spots + spot]]
+        for quarter in range(RING):
+            for half in range(2):
+                for way in range(2):
+                    at = quarter * 32 + half * 16 + way * TILE
+                    mine[half, way, quarter, spot] = value[at : at + TILE, :]
+        return carry
+
+    lax.fori_loop(0, spots, lay_out, 0, unroll=4)
 
     def keep_x(way, value):
         x_part[way] = value
@@ -396,13 +426,36 @@
     for copy in crossed + spread:
         copy.wait_send()
 
-    whole[...] = work[...].reshape(whole.shape)
-    invert([whole], 32, functools.partial(eliminate, ahead=16))
-    out[...] = whole[pl.ds(pl.multiple_of(x * rows, rows), rows), :]
-    for g in range(GROUPS):
+    out[...] = work[...].reshape(out.shape)
+    for piece in range(1, len(PIECES)):
         for kind in range(4):
-            gather(kind, g).wait_send()
+            gather(kind, piece).wait_send()
+    send_row.wait_send()
     for copy in stores + [store_inner]:
+        copy.wait()
+
+
+def deliver(inner, factor, reduced, inner_out, factor_out, own_out, held_inner, held_factor, whole, load, store):
+    part = factor.shape[0] // PARTS
+    moves = [(inner, held_inner, inner_out)]
+    for k in range(PARTS):
+        members = pl.ds(k * part, part)
+        moves.append((factor.at[members], held_factor.at[members], factor_out.at[members]))
+    loads = [pltpu.make_async_copy(here, held, load.at[k]) for k, (here, held, _) in enumerate(moves)]
+    stores = [pltpu.make_async_copy(held, there, store.at[k]) for k, (_, held, there) in enumerate(moves)]
+    for copy in loads:
+        copy.start()
+
+    def store_all():
+        for arrived, copy in zip(loads, stores):
+            arrived.wait()
+            copy.start()
+
+    whole[...] = reduced[...]
+    invert([whole], 32, functools.partial(eliminate, ahead=16), store_all)
+    rows = own_out.shape[0]
+    own_out[...] = whole[pl.ds(pl.multiple_of(lax.axis_index("cols") * rows, rows), rows), :]
+    for copy in stores:
         copy.wait()
 
 
@@ -417,24 +470,28 @@
     block = (size, size)
     dma = pltpu.SemaphoreType.DMA
     vmem = lambda *shape: pltpu.VMEM(shape, f32)
-    inner_inverse, lower_factor, own = pl.pallas_call(
+    inner_inverse, lower_factor, reduced = pl.pallas_call(
         kernel,
         out_shape=[
             jax.ShapeDtypeStruct(inner_pivots.shape, f32),
             jax.ShapeDtypeStruct(lower_blocks.shape, f32),
-            jax.ShapeDtypeStruct((rows, size), f32),
+            jax.ShapeDtypeStruct(block, f32),
         ],
-        in_specs=[SMEM, VMEM, SMEM, ANY, ANY, ANY, VMEM],
+        in_specs=[HBM] * 7,
         out_specs=[ANY, ANY, VMEM],
         scratch_shapes=[
+            pltpu.SMEM((couplings,), jnp.int32),
+            pltpu.VMEM((1, couplings), jnp.int32),
+            pltpu.VMEM((1, couplings), jnp.int32),
+            pltpu.SMEM((couplings,), jnp.int32),
+            vmem(rows, size),
             vmem(RING, count, *block),
             vmem(couplings, *block),
             vmem(couplings, *block),
             vmem(couplings, *block),
             vmem(couplings + 1, *block),
-            pltpu.SMEM((couplings + separators,), jnp.int32),
-            vmem(2, 2, RING, spots, *tile),
-            vmem(2, 2, RING, spots, *tile),
+            vmem(couplings + 1, *block),
+            pltpu.SMEM((couplings + 2 * spots,), jnp.int32),
             vmem(2, 2, RING, spots, *tile),
             vmem(6, spots, *tile),
             vmem(6, RING, DEPTH, *tile),
@@ -445,17 +502,20 @@
             vmem(DEPTH, 4, *tile),
             vmem(DEPTH - 1, 4, *tile),
             vmem(RING, rows, size),
-            vmem(*block),
-            dma((GROUPS,)),
+            vmem(PIECES[1][1], *block),
+            dma((4,)),
+            dma,
             dma((2, RING)),
-            dma((4, GROUPS)),
-            dma((4, GROUPS)),
+            dma((4, len(PIECES))),
+            dma((4, len(PIECES))),
             dma,
-            dma((5 * GROUPS,)),
+            dma((len(BLOCKS),)),
+            dma((len(BLOCKS),)),
+            dma((len(BLOCKS),)),
+            dma,
+            dma,
             dma((4, 6)),
             dma((4, 6)),
-            dma((4,)),
-            dma((4,)),
             dma((DEPTH - 1,)),
             dma((DEPTH - 1,)),
             dma((RING - 1,)),
@@ -471,6 +531,24 @@
         upper_blocks,
         separator_pivots[0],
     )
+    inner_inverse, lower_factor, own = pl.pallas_call(
+        deliver,
+        out_shape=[
+            jax.ShapeDtypeStruct(inner_pivots.shape, f32),
+            jax.ShapeDtypeStruct(lower_blocks.shape, f32),
+            jax.ShapeDtypeStruct((rows, size), f32),
+        ],
+        in_specs=[ANY, ANY, VMEM],
+        out_specs=[HBM, HBM, VMEM],
+        scratch_shapes=[
+            vmem(*inner_pivots.shape),
+            vmem(*lower_blocks.shape),
+            vmem(*block),
+            dma((PARTS + 1,)),
+            dma((PARTS + 1,)),
+        ],
+        compiler_params=pltpu.CompilerParams(vmem_limit_bytes=GRANT),
+    )(inner_inverse, lower_factor, reduced)
     return inner_inverse, lower_factor, own[None]
 
 

time: 85.1 us -> 74.7 us (0.88)
  local copies, waits for them, and re-layouts: 6.3 us -> 0 us
  Pallas kernels: 78 us -> 73.6 us
    pallas_call x1, Pallas kernels: 78 us -> 67.6 us  [shards(): pl.pallas_call(kernel, out_shape=[jax.ShapeDtypeStruct(inner_pivots.shape...]
    unnamed x11 -> x0, local copies, waits for them, and re-layouts: 6.3 us -> none
    pallas_call x0 -> x1, Pallas kernels: none -> 6.03 us  [shards(): pl.pallas_call(deliver, out_shape=[jax.ShapeDtypeStruct(inner_pivots.shap...]
where the time goes in v3:
time: 74.7 us; the launch traced here: 74.4 us
  Pallas kernels  73.6 us (99%)
  between operations  0.8 us (1%)
    pallas_call x1, Pallas kernels, shards(): pl.pallas_call(kernel, out_shape=[jax.ShapeDtypeStruct(inner_pivots.shape...  67.6 us
    pallas_call x1, Pallas kernels, shards(): pl.pallas_call(deliver, out_shape=[jax.ShapeDtypeStruct(inner_pivots.shap...  6.03 us

profile of v3, /device:TPU:2, one launch (start us, length us, event | category | flops | bytes accessed | tf_op | source)
XLA Modules:
  0.0 74.4 jit_solution(18078570471591807543)
XLA Ops:
  0.6 67.6 %shard_map.85 = (f32[12,128,128]{2,1,0:T(8,128)}, f32[48,1,128,128]{3,2,1,0:T(8,128)}, f32[128,128]{1,0:T(8,128)}) custom-call(s32[48]{0:T(128)} %bitcast.5, s32[1,48]{1,0:T(1,128)} %bitcast.6, s32[48]{0:T(128)} %counts_hbm.1, f32[12,128,128]{2,1,0:T(8,128)} %pivots.1, f32[48,1,128,128]{3,2,1,0:T(8,128)} %lower.1, f32[48,1,128,128]{3,2,1,0:T(8,128)} %upper.1, ...), custom_call_target="tpu_custom_call" | custom-call | tf_op jit(solution)/shard_map/pallas_call | solution.py:473
  68.2 6.0 %shard_map.86 = (f32[12,128,128]{2,1,0:T(8,128)}, f32[48,1,128,128]{3,2,1,0:T(8,128)}, f32[32,128]{1,0:T(8,128)}) custom-call(f32[12,128,128]{2,1,0:T(8,128)} %get-tuple-element.9.inner, f32[48,1,128,128]{3,2,1,0:T(8,128)} %get-tuple-element.10.factor, f32[128,128]{1,0:T(8,128)} %get-tuple-element.11.reduced), custom_call_target="tpu_custom_call" | custom-call | tf_op jit(solution)/shard_map/pallas_call | solution.py:534

commit v4 on v3

--- a/solution.py
+++ b/solution.py
@@ -88,7 +88,7 @@
             update = dot(whole[:, first : first + panel], slab)
             ref[...] = jnp.where(inside, 0.0, whole) - update
             ref[first : first + panel, :] = slab
-        if first == 0 and after_first is not None:
+        if first == panel and after_first is not None:
             after_first()
 
 

time: 74.7 us -> 73.9 us (0.989)
  Pallas kernels: 73.6 us -> 72.8 us
    pallas_call x1, Pallas kernels: 6.03 us -> 5.17 us  [shards(): pl.pallas_call(deliver, out_shape=[jax.ShapeDtypeStruct(inner_pivots.shap...]
where the time goes in v4:
time: 73.9 us; the launch traced here: 73.6 us
  Pallas kernels  72.8 us (99%)
  between operations  0.8 us (1%)
    pallas_call x1, Pallas kernels, shards(): pl.pallas_call(kernel, out_shape=[jax.ShapeDtypeStruct(inner_pivots.shape...  67.6 us
    pallas_call x1, Pallas kernels, shards(): pl.pallas_call(deliver, out_shape=[jax.ShapeDtypeStruct(inner_pivots.shap...  5.17 us

profile of v4, /device:TPU:2, one launch (start us, length us, event | category | flops | bytes accessed | tf_op | source)
XLA Modules:
  0.0 73.6 jit_solution(11222948022240407155)
XLA Ops:
  0.6 67.6 %shard_map.85 = (f32[12,128,128]{2,1,0:T(8,128)}, f32[48,1,128,128]{3,2,1,0:T(8,128)}, f32[128,128]{1,0:T(8,128)}) custom-call(s32[48]{0:T(128)} %bitcast.5, s32[1,48]{1,0:T(1,128)} %bitcast.6, s32[48]{0:T(128)} %counts_hbm.1, f32[12,128,128]{2,1,0:T(8,128)} %pivots.1, f32[48,1,128,128]{3,2,1,0:T(8,128)} %lower.1, f32[48,1,128,128]{3,2,1,0:T(8,128)} %upper.1, ...), custom_call_target="tpu_custom_call" | custom-call | tf_op jit(solution)/shard_map/pallas_call | solution.py:473
  68.2 5.2 %shard_map.86 = (f32[12,128,128]{2,1,0:T(8,128)}, f32[48,1,128,128]{3,2,1,0:T(8,128)}, f32[32,128]{1,0:T(8,128)}) custom-call(f32[12,128,128]{2,1,0:T(8,128)} %get-tuple-element.9.inner, f32[48,1,128,128]{3,2,1,0:T(8,128)} %get-tuple-element.10.factor, f32[128,128]{1,0:T(8,128)} %get-tuple-element.11.reduced), custom_call_target="tpu_custom_call" | custom-call | tf_op jit(solution)/shard_map/pallas_call | solution.py:534
